TPU v7x, 32 devices: a whole 2x2x4 slice. The times are simulated.
32 devices in a mesh: layer: 4 (over x, core), dp: 8 (over z, y).
Axes of the slice: x: 2, y: 2, z: 4, core: 2. Of those that a mesh axis runs over, the one named last changes fastest.
Arguments:
- out_grads: bfloat16 [4, 128, 16384], P('layer', None, 'dp'), may hold values from -3 to 3
- in_acts: bfloat16 [4, 128, 4096], P('layer', None, 'dp'), may hold values from -3 to 3
- out_basis: bfloat16 [4, 16384, 16384], P('layer', None, 'dp'), may hold values from -0.046875 to 0.046875
- in_basis: bfloat16 [4, 4096, 4096], P('layer', None, 'dp'), may hold values from -0.09375 to 0.09375
- eigenvalues: bfloat16 [4, 16384, 4096], P('layer', 'dp'), may hold values from 0.5 to 50
- out_store: bfloat16 [4, 16, 32, 16384], P('layer', 'dp'), may hold values from -0.046875 to 0.046875
- in_store: bfloat16 [4, 16, 32, 4096], P('layer', 'dp'), may hold values from -0.09375 to 0.09375
- counts: int32 [16], P('dp'), may hold values from 1 to 4096
- winners: int32 [4, 6], replicated, may hold values from 0 to 15
Outputs:
- influence: float32 [4, 6, 32], replicated
All inputs are finite; a program needn't handle non-finite values.
Results may differ from a plain program's by a relative error of at most 0.0055.
Values may be sent and summed in bfloat16 or wider, within the bound.
A program may use at most 192 MiB of HBM per device.

v0:
```python
import jax
import jax.numpy as jnp
from jax import lax
from jax.sharding import PartitionSpec as P

NQ = 4
TQ = 32
WIN = 6
R = 32
SPAN = 128
damping = 0.1


def on_device(
    out_grads, in_acts, out_basis, in_basis, eigenvalues, out_store, in_store, counts, winners
):
    out_local = out_basis[0]
    in_local = in_basis[0]
    out_width = out_local.shape[1]
    rows = out_local
    turned_out = jnp.dot(
        lax.all_gather(out_grads[0], "dp", axis=1, tiled=True),
        rows,
        preferred_element_type=jnp.float32,
    ).astype(jnp.bfloat16)
    rows = in_local
    turned_part = jnp.dot(
        lax.all_gather(in_acts[0], "dp", axis=1, tiled=True),
        rows,
        preferred_element_type=jnp.float32,
    ).astype(jnp.bfloat16)
    turned_in = lax.all_gather(turned_part, "dp", axis=1, tiled=True)
    left = turned_out.reshape(NQ, TQ, out_width)
    right = turned_in.reshape(NQ, TQ, turned_in.shape[1])
    product = jnp.einsum("qtf,qtd->qfd", left, right, preferred_element_type=jnp.float32)
    divisor = eigenvalues[0].astype(jnp.float32) + damping
    precond = (product / divisor[None]).astype(jnp.bfloat16)
    alive = (jnp.arange(R, dtype=jnp.int32)[None, :] * SPAN < counts[:, None]).astype(jnp.bfloat16)
    masked = in_store[0] * alive[:, :, None]
    out_slices = lax.all_to_all(out_store[0], "dp", split_axis=2, concat_axis=0, tiled=True)
    chosen = winners.reshape(NQ * WIN)
    left_rows = jnp.take(out_slices, chosen, axis=0).reshape(NQ, WIN * R, out_width)
    full_width = turned_in.shape[1]
    in_whole = lax.all_gather(masked, "dp", axis=0, tiled=True)
    right_rows = jnp.take(in_whole, chosen, axis=0).reshape(NQ, WIN * R, full_width)
    mapped = jnp.einsum("qfd,qkd->qkf", precond, right_rows, preferred_element_type=jnp.float32)
    partial_value = jnp.sum(mapped * left_rows.astype(jnp.float32), axis=2)
    totals = lax.psum(partial_value, ("layer", "dp"))
    return totals.reshape(NQ, WIN, R)


def solution(mesh):
    placed = (
        P("layer", None, "dp"),
        P("layer", None, "dp"),
        P("layer", None, "dp"),
        P("layer", None, "dp"),
        P("layer", "dp", None),
        P("layer", "dp", None, None),
        P("layer", "dp", None, None),
        P("dp"),
        P(),
    )
    return jax.shard_map(on_device, mesh=mesh, in_specs=placed, out_specs=P(), check_vma=False)
```

profile of v0, /device:TPU:0, one launch (start us, length us, event | category | flops | bytes accessed | tf_op | source)
XLA Modules:
  0.0 364.3 jit_solution(16281501123913025915)
XLA Ops:
  6.5 0.7 all-gather.13.cloned.1.call-update
  7.3 0.0 all-gather.11.cloned.1.call-start
  7.3 0.7 all-gather.11.cloned.1.call-update
  8.0 0.0 all-gather.7.cloned.1.call-start
  8.1 0.7 compare_convert_fusion
  8.8 2.0 bitcast_multiply_fusion
  10.7 0.0 all-gather.7.cloned.1.call-update
  10.8 17.2 %copy.13 = bf16[1,2,32,16384]{2,1,3,0:T(2,128)(2,1)} copy(bf16[1,2,32,16384]{3,2,1,0:T(8,128)(2,1)} %param.14) | data formatting | bytes 4194304 | tf_op args[5]
  28.0 8.0 %bitcast_bitcast_fusion = bf16[16384,2,32]{2,1,0:T(2,128)(2,1)} fusion(bf16[1,2,32,16384]{2,1,3,0:T(2,128)(2,1)} %copy.13), kind=kLoop, calls=%fused_computation.25 | loop fusion | bytes 4194304
  36.0 11.2 %reshape.112 = bf16[8,2,65536]{2,1,0:T(2,128)(2,1)} reshape(bf16[16384,2,32]{2,1,0:T(2,128)(2,1)} %bitcast_bitcast_fusion) | data formatting | bytes 4194304
  47.2 7.3 %all-to-all-start = ((bf16[8,2,65536]{2,1,0:T(2,128)(2,1)}), bf16[8,2,65536]{2,1,0:T(2,128)(2,1)S(1)}, u32[]{:S(2)}, u32[]{:S(2)}) async-start(bf16[8,2,65536]{2,1,0:T(2,128)(2,1)} %reshape.112), calls=%async_computation | async-start | bytes 4194304 | tf_op jit(solution)/shard_map/all_to_all | solution.py:40
  54.5 0.0 all-gather.9.cloned.1.call-start
  54.6 0.1 reshape.90
  54.7 0.1 broadcast_in_dim.28
  54.8 0.1 broadcast_in_dim.29
  54.9 18.8 %add_bitcast_fusion = f32[2048,4096]{1,0:T(8,128)} fusion(bf16[1,2048,4096]{2,1,0:T(8,128)(2,1)} %param.13), kind=kLoop, calls=%fused_computation.6 | loop fusion | flops 16777216 | bytes 50331648 | tf_op jit(solution)/shard_map/div | solution.py:37
  73.7 3.9 %fusion.13 = bf16[128,512]{1,0:T(8,128)(2,1)} fusion(bf16[1,4096,512]{2,1,0:T(8,128)(2,1)} %param.12, bf16[1,128,4096]{2,1,0:T(8,128)(2,1)} %all-gather.13.cloned.1.call-done), kind=kOutput, calls=%fused_computation.15 | convolution fusion | flops 536936448 | bytes 5373952 | tf_op jit(solution)/shard_map/dot_general | solution.py:27
  77.6 0.0 all-gather.9.cloned.1.call-update
  77.6 50.9 %all-to-all-done = bf16[8,2,65536]{2,1,0:T(2,128)(2,1)S(1)} async-done(((bf16[8,2,65536]{2,1,0:T(2,128)(2,1)}), bf16[8,2,65536]{2,1,0:T(2,128)(2,1)S(1)}, u32[]{:S(2)}, u32[]{:S(2)}) %all-to-all-start) | async-done | bytes 2097184 | tf_op jit(solution)/shard_map/all_to_all | solution.py:40
  128.5 6.5 %reshape.113 = bf16[16384,2,32]{2,1,0:T(2,128)(2,1)} reshape(bf16[8,2,65536]{2,1,0:T(2,128)(2,1)S(1)} %all-to-all-done) | data formatting | bytes 4194304
  135.0 17.8 %copy.18 = bf16[2,32,8,2048]{3,1,0,2:T(8,128)(2,1)S(1)} copy(bf16[2,32,8,2048]{1,0,3,2:T(2,128)(2,1)} %bitcast.47) | data formatting | bytes 4194304 | tf_op jit(solution)/shard_map/all_to_all | solution.py:40
  152.8 2.5 gather_fusion.1
  155.3 26.3 %fusion.8 = bf16[128,2048]{1,0:T(8,128)(2,1)} fusion(bf16[1,16384,2048]{2,1,0:T(8,128)(2,1)} %param.11, bf16[1,128,16384]{2,1,0:T(8,128)(2,1)} %all-gather.11.cloned.1.call-done), kind=kOutput, calls=%fused_computation.14 | convolution fusion | flops 8590196736 | bytes 71827456 | tf_op jit(solution)/shard_map/dot_general | solution.py:21
  181.5 46.3 %all-gather.7.cloned.1.call-done = bf16[16,32,4096]{2,1,0:T(8,128)(2,1)} async-done(((bf16[2,32,4096]{2,1,0:T(8,128)(2,1)}), bf16[16,32,4096]{2,1,0:T(8,128)(2,1)}) %all-gather.7.cloned.1.call-update) | async-done | bytes 4194320 | tf_op jit(solution)/shard_map/all_gather | solution.py:44
  227.8 6.5 %gather_fusion = bf16[24,32,4096]{2,1,0:T(8,128)(2,1)} fusion(bf16[16,32,4096]{2,1,0:T(8,128)(2,1)} %all-gather.7.cloned.1.call-done, s32[1024]{0:T(1024)S(1)} %pad_clamp_fusion), kind=kCustom, calls=%fused_computation | custom fusion | bytes 12583008 | tf_op jit(solution)/shard_map/jit(_take)/gather | solution.py:45
  234.3 6.1 %bitcast_select_fusion = bf16[4,192,4096]{2,1,0:T(8,128)(2,1)} fusion(pred[4,192]{1,0:T(4,128)(4,1)S(1)} %broadcast_in_dim.29, bf16[4,192,4096]{2,1,0:T(8,128)(2,1)} %bitcast.48), kind=kLoop, calls=%fused_computation.8 | loop fusion | flops 3145728 | bytes 12583680 | tf_op jit(solution)/shard_map/jit(_take)/select_n | solution.py:45
  240.5 27.2 %all-gather.9.cloned.1.call-done = bf16[128,4096]{1,0:T(8,128)(2,1)} async-done(((bf16[128,512]{1,0:T(8,128)(2,1)}), bf16[128,4096]{1,0:T(8,128)(2,1)}) %all-gather.9.cloned.1.call-update) | async-done | bytes 1048592 | tf_op jit(solution)/shard_map/all_gather | solution.py:32
  267.7 45.8 %fusion.2 = f32[4,192,2048]{2,1,0:T(8,128)} fusion(bf16[4,192,4096]{2,1,0:T(8,128)(2,1)} %bitcast_select_fusion, f32[2048,4096]{1,0:T(8,128)} %add_bitcast_fusion, bf16[4,32,2048]{2,1,0:T(8,128)(2,1)} %bitcast.51, bf16[4,32,4096]{2,1,0:T(8,128)(2,1)} %bitcast.52), kind=kOutput, calls=%fused_computation.5 | convolution fusion | flops 15099494400 | bytes 47710208 | tf_op jit(solution)/shard_map/qfd,qkd->qkf/dot_general | solution.py:46
  313.5 3.8 %multiply_reduce_fusion = f32[4,192]{1,0:T(4,128)S(1)} fusion(f32[4,192,2048]{2,1,0:T(8,128)} %fusion.2, pred[4,192]{1,0:T(4,128)(4,1)S(1)} %broadcast_in_dim.29, bf16[4,192,2048]{2,1,0:T(8,128)(2,1)S(1)} %bitcast.50), kind=kLoop, calls=%fused_computation.9 | loop fusion | flops 6290688 | bytes 9441024 | tf_op jit(solution)/shard_map/reduce_sum | solution.py:47
  317.3 0.1 reshape.93
  317.4 39.8 %psum.7 = f32[4,6,32]{2,1,0:T(8,128)S(1)} all-reduce(f32[4,6,32]{2,1,0:T(8,128)S(1)} %reshape.93), channel_id=1, replica_groups=mesh['layer'=4,'dp'=8] {'layer','dp'}, use_global_device_ids=true, to_apply=%region_1.2 | all-reduce | flops 768 | bytes 6144 | tf_op jit(solution)/shard_map/psum | solution.py:48
  357.2 0.6 copy.16
  (11 shorter events, 0.0 us)
Async XLA Ops:
  6.5 67.1 %all-gather.13.cloned.1.call-start = ((), (), s32[]{:S(2)}) async-start(), calls=%async_computation.4 | async-start | bytes 1179648 | tf_op jit(solution)/shard_map/all_gather | solution.py:28
  7.3 148.0 %all-gather.11.cloned.1.call-start = ((), (), s32[]{:S(2)}) async-start(), calls=%async_computation.3 | async-start | bytes 4718592 | tf_op jit(solution)/shard_map/all_gather | solution.py:22
  8.0 219.8 %all-gather.7.cloned.1.call-start = ((), (), s32[]{:S(2)}) async-start(), calls=%async_computation.1 | async-start | bytes 4718592 | tf_op jit(solution)/shard_map/all_gather | solution.py:44
  36.0 18.6 %copy-start.1 = (s32[4,6]{1,0:T(4,128)S(1)}, s32[4,6]{1,0:T(4,128)}, u32[]{:S(2)}) copy-start(s32[4,6]{1,0:T(4,128)} %param.17) | copy-start | bytes 292
  47.2 81.3 %all-to-all-start = ((bf16[8,2,65536]{2,1,0:T(2,128)(2,1)}), bf16[8,2,65536]{2,1,0:T(2,128)(2,1)S(1)}, u32[]{:S(2)}, u32[]{:S(2)}) async-start(bf16[8,2,65536]{2,1,0:T(2,128)(2,1)} %reshape.112), calls=%async_computation | async-start | bytes 4194304 | tf_op jit(solution)/shard_map/all_to_all | solution.py:40
  54.5 213.1 %all-gather.9.cloned.1.call-start = ((), (), s32[]{:S(2)}) async-start(), calls=%async_computation.2 | async-start | bytes 1179648 | tf_op jit(solution)/shard_map/all_gather | solution.py:32
  267.7 45.8 %copy-start = (bf16[24,32,2048]{2,1,0:T(8,128)(2,1)S(1)}, bf16[24,32,2048]{2,1,0:T(8,128)(2,1)}, u32[]{:S(2)}) copy-start(bf16[24,32,2048]{2,1,0:T(8,128)(2,1)} %gather_fusion.1) | copy-start | bytes 9437188
Sparse Core Ops, SparseCore 0:
  9.4 42.1 all-gather.12
  53.7 100.1 all-gather.10
  156.0 71.7 all-gather.6
  229.7 37.9 all-gather.8
where the time goes:
time: 366 us; the launch traced here: 364 us
  waiting for transfers between devices  126 us (34%)
  matrix products  76 us (21%)
  local copies, waits for them, and re-layouts  70.7 us (19%)
  blocking collectives  39.8 us (11%)
  other arithmetic  31.4 us (9%)
  between operations  13.2 us (4%)
  starting transfers between devices  7.43 us (2%)
    all_to_all x1, waiting for transfers between devices, on_device(): lax.all_to_all(out_store[0], 'dp', split_axis=2, concat_axis=0, tiled=True)  50.9 us
    all_gather x1, waiting for transfers between devices, on_device(): in_whole = lax.all_gather(masked, 'dp', axis=0, tiled=True)  46.3 us
    dot_general x1, matrix products, on_device(): jnp.einsum('qfd,qkd->qkf', precond, right_rows, preferred_element_type=jn...  45.8 us
    unnamed x8, local copies, waits for them, and re-layouts  43 us
    psum x1, blocking collectives, on_device(): totals = lax.psum(partial_value, ('layer', 'dp'))  39.8 us
    all_gather x1, waiting for transfers between devices, on_device(): turned_in = lax.all_gather(turned_part, 'dp', axis=1, tiled=True)  27.2 us
    dot_general x1, matrix products, on_device(): jnp.dot(lax.all_gather(out_grads[0], 'dp', axis=1, tiled=True), rows, pre...  26.3 us
    div x1, other arithmetic, on_device(): precond = (product / divisor[None]).astype(jnp.bfloat16)  18.8 us
  transfers between devices with their start and end apart: 5, of which 3 were waited for; matrix products, arithmetic and copies ran while one was open for 35% of the time, Pallas kernels for 0%

commit v1 on v0

--- a/solution.py
+++ b/solution.py
@@ -37,7 +37,11 @@
     precond = (product / divisor[None]).astype(jnp.bfloat16)
     alive = (jnp.arange(R, dtype=jnp.int32)[None, :] * SPAN < counts[:, None]).astype(jnp.bfloat16)
     masked = in_store[0] * alive[:, :, None]
-    out_slices = lax.all_to_all(out_store[0], "dp", split_axis=2, concat_axis=0, tiled=True)
+    own = out_store[0]
+    size = lax.axis_size("dp")
+    blocks = jnp.stack(jnp.split(own, size, axis=2), axis=0)
+    blocks = lax.all_to_all(blocks, "dp", split_axis=0, concat_axis=0)
+    out_slices = jnp.concatenate(blocks, axis=0)
     chosen = winners.reshape(NQ * WIN)
     left_rows = jnp.take(out_slices, chosen, axis=0).reshape(NQ, WIN * R, out_width)
     full_width = turned_in.shape[1]

time: 366 us -> 367 us (level)
  waiting for transfers between devices: 126 us -> 181 us
  local copies, waits for them, and re-layouts: 70.7 us -> 17.6 us
    all_gather x1, waiting for transfers between devices: 0.01 us -> 69.3 us  [on_device(): lax.all_gather(out_grads[0], 'dp', axis=1, tiled=True)]
    all_to_all x1, waiting for transfers between devices: 50.9 us -> 2.02 us  [on_device(): blocks = lax.all_to_all(blocks, 'dp', split_axis=0, concat_axis=0)]
    unnamed x8 -> x13, local copies, waits for them, and re-layouts: 43 us -> 6.98 us
    all_gather x1, waiting for transfers between devices: 0.01 us -> 33.5 us  [on_device(): lax.all_gather(in_acts[0], 'dp', axis=1, tiled=True)]
    all_to_all x1 -> x0, local copies, waits for them, and re-layouts: 17.8 us -> none  [on_device(): lax.all_to_all(out_store[0], 'dp', split_axis=2, concat_axis=0, tiled=True)]
  transfers between devices with their start and end apart: 5 -> 5, of which waited for: 3 -> 5; matrix products, arithmetic and copies ran while one was open for 35% -> 20% of each run, Pallas kernels for 0% -> 0%
where the time goes in v1:
time: 367 us; the launch traced here: 366 us
  waiting for transfers between devices  181 us (49%)
  matrix products  75.9 us (21%)
  blocking collectives  39.9 us (11%)
  other arithmetic  31.3 us (9%)
  local copies, waits for them, and re-layouts  17.6 us (5%)
  between operations  13.2 us (4%)
  starting transfers between devices  7.42 us (2%)
    all_gather x1, waiting for transfers between devices, on_device(): lax.all_gather(out_grads[0], 'dp', axis=1, tiled=True)  69.3 us
    all_gather x1, waiting for transfers between devices, on_device(): in_whole = lax.all_gather(masked, 'dp', axis=0, tiled=True)  47.2 us
    dot_general x1, matrix products, on_device(): jnp.einsum('qfd,qkd->qkf', precond, right_rows, preferred_element_type=jn...  45.8 us
    psum x1, blocking collectives, on_device(): totals = lax.psum(partial_value, ('layer', 'dp'))  39.9 us
    all_gather x1, waiting for transfers between devices, on_device(): lax.all_gather(in_acts[0], 'dp', axis=1, tiled=True)  33.5 us
    all_gather x1, waiting for transfers between devices, on_device(): turned_in = lax.all_gather(turned_part, 'dp', axis=1, tiled=True)  27.2 us
    dot_general x1, matrix products, on_device(): jnp.dot(lax.all_gather(out_grads[0], 'dp', axis=1, tiled=True), rows, pre...  26.2 us
    div x1, other arithmetic, on_device(): precond = (product / divisor[None]).astype(jnp.bfloat16)  18.7 us
  transfers between devices with their start and end apart: 5, of which 5 were waited for; matrix products, arithmetic and copies ran while one was open for 20% of the time, Pallas kernels for 0%

profile of v1, /device:TPU:0, one launch (start us, length us, event | category | flops | bytes accessed | tf_op | source)
XLA Modules:
  0.0 366.0 jit_solution(10151527656305338172)
XLA Ops:
  6.5 0.7 all-gather.13.cloned.1.call-update
  7.3 0.7 all-gather.11.cloned.1.call-update
  8.1 0.7 compare_convert_fusion
  8.8 1.9 bitcast_multiply_fusion
  10.8 1.7 fusion.24
  12.4 1.7 fusion.23
  14.1 0.7 fusion.22
  14.8 0.7 fusion.21
  15.5 0.7 fusion.20
  16.3 0.7 fusion.19
  17.0 0.7 fusion.18
  17.7 0.7 fusion.17
  18.5 7.3 %all-to-all-start = ((bf16[8,2,32,2048]{3,2,1,0:T(8,128)(2,1)}), bf16[8,2,32,2048]{3,2,1,0:T(8,128)(2,1)S(1)}, u32[]{:S(2)}, u32[]{:S(2)}) async-start(bf16[8,2,32,2048]{3,2,1,0:T(8,128)(2,1)} %fusion.17), calls=%async_computation | async-start | bytes 4194304 | tf_op jit(solution)/shard_map/all_to_all | solution.py:43
  25.8 0.1 reshape.93
  25.9 0.1 broadcast_in_dim.28
  26.0 0.1 broadcast_in_dim.29
  26.1 18.7 %add_bitcast_fusion = f32[2048,4096]{1,0:T(8,128)} fusion(bf16[1,2048,4096]{2,1,0:T(8,128)(2,1)} %param.13), kind=kLoop, calls=%fused_computation.6 | loop fusion | flops 16777216 | bytes 50331648 | tf_op jit(solution)/shard_map/div | solution.py:37
  44.8 33.5 %all-gather.13.cloned.1.call-done = bf16[1,128,4096]{2,1,0:T(8,128)(2,1)} async-done(((bf16[1,128,512]{2,1,0:T(8,128)(2,1)}), bf16[1,128,4096]{2,1,0:T(8,128)(2,1)}) %all-gather.13.cloned.1.call-update) | async-done | bytes 1048592 | tf_op jit(solution)/shard_map/all_gather | solution.py:28
  78.3 3.9 %fusion.13 = bf16[128,512]{1,0:T(8,128)(2,1)} fusion(bf16[1,4096,512]{2,1,0:T(8,128)(2,1)} %param.12, bf16[1,128,4096]{2,1,0:T(8,128)(2,1)} %all-gather.13.cloned.1.call-done), kind=kOutput, calls=%fused_computation.15 | convolution fusion | flops 536936448 | bytes 5373952 | tf_op jit(solution)/shard_map/dot_general | solution.py:27
  82.2 2.0 all-to-all-done
  84.2 2.5 gather_fusion.1
  86.7 69.3 %all-gather.11.cloned.1.call-done = bf16[1,128,16384]{2,1,0:T(8,128)(2,1)} async-done(((bf16[1,128,2048]{2,1,0:T(8,128)(2,1)}), bf16[1,128,16384]{2,1,0:T(8,128)(2,1)}) %all-gather.11.cloned.1.call-update) | async-done | bytes 4194320 | tf_op jit(solution)/shard_map/all_gather | solution.py:22
  156.0 26.2 %fusion.8 = bf16[128,2048]{1,0:T(8,128)(2,1)} fusion(bf16[1,16384,2048]{2,1,0:T(8,128)(2,1)} %param.11, bf16[1,128,16384]{2,1,0:T(8,128)(2,1)} %all-gather.11.cloned.1.call-done), kind=kOutput, calls=%fused_computation.14 | convolution fusion | flops 8590196736 | bytes 71827456 | tf_op jit(solution)/shard_map/dot_general | solution.py:21
  182.3 47.2 %all-gather.7.cloned.1.call-done = bf16[16,32,4096]{2,1,0:T(8,128)(2,1)} async-done(((bf16[2,32,4096]{2,1,0:T(8,128)(2,1)}), bf16[16,32,4096]{2,1,0:T(8,128)(2,1)}) %all-gather.7.cloned.1.call-update) | async-done | bytes 4194320 | tf_op jit(solution)/shard_map/all_gather | solution.py:48
  229.5 6.5 %gather_fusion = bf16[24,32,4096]{2,1,0:T(8,128)(2,1)} fusion(bf16[16,32,4096]{2,1,0:T(8,128)(2,1)} %all-gather.7.cloned.1.call-done, s32[1024]{0:T(1024)S(1)} %pad_clamp_fusion), kind=kCustom, calls=%fused_computation | custom fusion | bytes 12583008 | tf_op jit(solution)/shard_map/jit(_take)/gather | solution.py:49
  236.0 6.1 %bitcast_select_fusion = bf16[4,192,4096]{2,1,0:T(8,128)(2,1)} fusion(pred[4,192]{1,0:T(4,128)(4,1)S(1)} %broadcast_in_dim.29, bf16[4,192,4096]{2,1,0:T(8,128)(2,1)} %bitcast.71), kind=kLoop, calls=%fused_computation.8 | loop fusion | flops 3145728 | bytes 12583680 | tf_op jit(solution)/shard_map/jit(_take)/select_n | solution.py:49
  242.1 27.2 %all-gather.9.cloned.1.call-done = bf16[128,4096]{1,0:T(8,128)(2,1)} async-done(((bf16[128,512]{1,0:T(8,128)(2,1)}), bf16[128,4096]{1,0:T(8,128)(2,1)}) %all-gather.9.cloned.1.call-update) | async-done | bytes 1048592 | tf_op jit(solution)/shard_map/all_gather | solution.py:32
  269.4 45.8 %fusion.2 = f32[4,192,2048]{2,1,0:T(8,128)} fusion(bf16[4,192,4096]{2,1,0:T(8,128)(2,1)} %bitcast_select_fusion, f32[2048,4096]{1,0:T(8,128)} %add_bitcast_fusion, bf16[4,32,2048]{2,1,0:T(8,128)(2,1)} %bitcast.82, bf16[4,32,4096]{2,1,0:T(8,128)(2,1)} %bitcast.83), kind=kOutput, calls=%fused_computation.5 | convolution fusion | flops 15099494400 | bytes 47710208 | tf_op jit(solution)/shard_map/qfd,qkd->qkf/dot_general | solution.py:50
  315.2 3.8 %multiply_reduce_fusion = f32[4,192]{1,0:T(4,128)S(1)} fusion(f32[4,192,2048]{2,1,0:T(8,128)} %fusion.2, pred[4,192]{1,0:T(4,128)(4,1)S(1)} %broadcast_in_dim.29, bf16[4,192,2048]{2,1,0:T(8,128)(2,1)S(1)} %bitcast.73), kind=kLoop, calls=%fused_computation.9 | loop fusion | flops 6290688 | bytes 9441024 | tf_op jit(solution)/shard_map/reduce_sum | solution.py:51
  318.9 0.1 reshape.97
  319.0 39.9 %psum.7 = f32[4,6,32]{2,1,0:T(8,128)S(1)} all-reduce(f32[4,6,32]{2,1,0:T(8,128)S(1)} %reshape.97), channel_id=1, replica_groups=mesh['layer'=4,'dp'=8] {'layer','dp'}, use_global_device_ids=true, to_apply=%region_1.2 | all-reduce | flops 768 | bytes 6144 | tf_op jit(solution)/shard_map/psum | solution.py:52
  358.9 0.6 copy.11
  (16 shorter events, 0.2 us)
Async XLA Ops:
  6.5 7.6 %copy-start.1 = (bf16[1,2,32,16384]{3,2,1,0:T(8,128)(2,1)S(1)}, bf16[1,2,32,16384]{3,2,1,0:T(8,128)(2,1)}, u32[]{:S(2)}) copy-start(bf16[1,2,32,16384]{3,2,1,0:T(8,128)(2,1)} %param.14) | copy-start | bytes 6291460
  6.5 71.7 %all-gather.13.cloned.1.call-start = ((), (), s32[]{:S(2)}) async-start(), calls=%async_computation.4 | async-start | bytes 1179648 | tf_op jit(solution)/shard_map/all_gather | solution.py:28
  7.3 148.7 %all-gather.11.cloned.1.call-start = ((), (), s32[]{:S(2)}) async-start(), calls=%async_computation.3 | async-start | bytes 4718592 | tf_op jit(solution)/shard_map/all_gather | solution.py:22
  8.0 221.5 %all-gather.7.cloned.1.call-start = ((), (), s32[]{:S(2)}) async-start(), calls=%async_computation.1 | async-start | bytes 4718592 | tf_op jit(solution)/shard_map/all_gather | solution.py:48
  15.5 10.3 %copy-start.2 = (s32[4,6]{1,0:T(4,128)S(1)}, s32[4,6]{1,0:T(4,128)}, u32[]{:S(2)}) copy-start(s32[4,6]{1,0:T(4,128)} %param.17) | copy-start | bytes 292
  18.5 65.8 %all-to-all-start = ((bf16[8,2,32,2048]{3,2,1,0:T(8,128)(2,1)}), bf16[8,2,32,2048]{3,2,1,0:T(8,128)(2,1)S(1)}, u32[]{:S(2)}, u32[]{:S(2)}) async-start(bf16[8,2,32,2048]{3,2,1,0:T(8,128)(2,1)} %fusion.17), calls=%async_computation | async-start | bytes 4194304 | tf_op jit(solution)/shard_map/all_to_all | solution.py:43
  25.8 243.6 %all-gather.9.cloned.1.call-start = ((), (), s32[]{:S(2)}) async-start(), calls=%async_computation.2 | async-start | bytes 1179648 | tf_op jit(solution)/shard_map/all_gather | solution.py:32
  269.4 45.8 %copy-start = (bf16[24,32,2048]{2,1,0:T(8,128)(2,1)S(1)}, bf16[24,32,2048]{2,1,0:T(8,128)(2,1)}, u32[]{:S(2)}) copy-start(bf16[24,32,2048]{2,1,0:T(8,128)(2,1)} %gather_fusion.1) | copy-start | bytes 9437188
Sparse Core Ops, SparseCore 0:
  9.4 68.8 all-gather.12
  80.5 75.4 all-gather.10
  158.1 71.3 all-gather.6
  231.4 37.9 all-gather.8
